TPU v7x, 32 devices: a whole 2x2x4 slice. The times are simulated.
32 devices in a mesh: wide: 8 (over z, y), narrow: 4 (over x, core).
Axes of the slice: x: 2, y: 2, z: 4, core: 2. Of those that a mesh axis runs over, the one named last changes fastest.
Arguments:
- panel: float32 [16384, 128], P(('wide', 'narrow')), may hold values from -40 to 40
- trailing: float32 [16384, 256], P(('wide', 'narrow')), may hold values from -40 to 40
Outputs:
- q_factor: float32 [16384, 128], P(('wide', 'narrow'))
- r_factor: float32 [128, 128], replicated
- projection: float32 [128, 256], replicated
- updated: float32 [16384, 256], P(('wide', 'narrow'))
All inputs are finite; a program needn't handle non-finite values.
Results may differ from a plain program's by a relative error of at most 0.00045.
Values sent between devices are 32-bit elements; how exact they have to be, the bound alone decides.
No kernel may reach another device: no remote copies, remote signals or barrier semaphores. Data moves between devices by JAX's collectives and lax.ppermute only.
A program may use at most 64 MiB of HBM per device.

v0:
```python
import jax
import jax.numpy as jnp
from jax import lax
from jax.sharding import PartitionSpec as P


def upper_factor(gram_matrix):
    order = gram_matrix.shape[0]
    columns = jnp.arange(order, dtype=jnp.int32)

    def column_step(index, state):
        work, factor = state
        where = jnp.asarray(index).astype(jnp.int32)
        pivot_row = lax.dynamic_index_in_dim(work, where, 0, keepdims=False)
        pivot = lax.dynamic_index_in_dim(pivot_row, where, 0, keepdims=False)
        new_row = jnp.where(
            columns >= where, pivot_row / jnp.sqrt(pivot), jnp.zeros_like(pivot_row)
        )
        work = work - new_row[:, None] * new_row[None, :]
        factor = lax.dynamic_update_slice_in_dim(factor, new_row[None, :], where, 0)
        return (work, factor)

    start = (gram_matrix, jnp.zeros_like(gram_matrix))
    return lax.fori_loop(0, order, column_step, start)[1]


def inverse_upper(upper_part):
    order = upper_part.shape[0]
    identity = jnp.eye(order, dtype=upper_part.dtype)

    def row_step(count, inverse):
        where = (order - 1 - jnp.asarray(count)).astype(jnp.int32)
        upper_row = lax.dynamic_index_in_dim(upper_part, where, 0, keepdims=False)
        unit_row = lax.dynamic_index_in_dim(identity, where, 0, keepdims=False)
        pivot = lax.dynamic_index_in_dim(upper_row, where, 0, keepdims=False)
        partial_value = jnp.dot(upper_row, inverse, precision=lax.Precision.HIGHEST)
        new_row = (unit_row - partial_value) / pivot
        return lax.dynamic_update_slice_in_dim(inverse, new_row[None, :], where, 0)

    return lax.fori_loop(0, order, row_step, jnp.zeros_like(upper_part))


def product(left, right):
    return jnp.dot(left, right, precision=lax.Precision.HIGHEST, preferred_element_type=jnp.float32)


def on_device(panel, trailing):
    row_total = float(panel.shape[0] * lax.axis_size("wide") * lax.axis_size("narrow"))
    gram_local = product(panel.T, panel) / row_total
    cross_local = product(panel.T, trailing) / row_total
    gram_first, cross_terms = lax.psum((gram_local, cross_local), ("wide", "narrow"))
    first_factor = upper_factor(gram_first)
    basis_rows = product(panel, inverse_upper(first_factor))
    gram_second = lax.psum(product(basis_rows.T, basis_rows) / row_total, ("wide", "narrow"))
    second_factor = upper_factor(gram_second)
    q_factor = product(basis_rows, inverse_upper(second_factor))
    r_factor = product(second_factor, first_factor)
    projection = product(inverse_upper(r_factor).T, cross_terms)
    updated = trailing - product(q_factor, projection)
    return (q_factor, r_factor, projection, updated)


def solution(mesh):
    in_specs = (P(("wide", "narrow"), None), P(("wide", "narrow"), None))
    out_specs = (P(("wide", "narrow"), None), P(), P(), P(("wide", "narrow"), None))
    return jax.shard_map(
        on_device, mesh=mesh, in_specs=in_specs, out_specs=out_specs, check_vma=False
    )
```

profile of v0, /device:TPU:8, one launch (start us, length us, event | category | flops | bytes accessed | tf_op | source)
XLA Modules:
  0.0 1208.6 jit_solution(7260193359423582820)
XLA Ops:
  7.2 0.9 copy-done
  8.1 1.2 convolution_multiply_fusion.2
  9.4 1.3 convolution_multiply_fusion
  10.7 125.4 %all-reduce.4.cloned.1.call-done = f32[128,128]{1,0:T(8,128)} async-done(((f32[128,128]{1,0:T(8,128)}), f32[128,128]{1,0:T(8,128)}) %all-reduce.4.cloned.1.call-update) | async-done | bytes 65552 | tf_op jit(solution)/shard_map/psum | solution.py:51
  136.1 0.8 copy-done.3
  137.0 188.3 %while.89 = (s32[]{:T(128)}, f32[128,128]{1,0:T(8,128)S(1)}, f32[128,128]{1,0:T(8,128)S(1)}, s32[]{:T(128)}, s32[]{:T(128)}, /*index=5*/s32[]{:T(128)}) while((s32[]{:T(128)}, f32[128,128]{1,0:T(8,128)S(1)}, f32[128,128]{1,0:T(8,128)S(1)}, s32[]{:T(128)}, s32[]{:T(128)}, /*index=5*/s32[]{:T(128)}) %tuple.212), condition=%wide.region_2.3_spmd.clone, body=%wide.region_1.0_spmd.clone.sunk | while | flops 33667 | bytes 138357 | solution.py:24
  325.2 185.2 %while.86 = (s32[]{:T(128)}, f32[128,128]{1,0:T(8,128)S(1)}, f32[128,128]{1,0:T(8,128)S(1)}, f32[128,128]{1,0:T(8,128)S(1)}, s32[]{:T(128)}, /*index=5*/s32[]{:T(128)}, s32[]{:T(128)}, s32[]{:T(128)}) while((s32[]{:T(128)}, f32[128,128]{1,0:T(8,128)S(1)}, f32[128,128]{1,0:T(8,128)S(1)}, f32[128,128]{1,0:T(8,128)S(1)}, s32[]{:T(128)}, ...), condition=%wide.region_4.5_spmd, body=%wide.region_3.4_spmd.sunk | while | flops 196871 | bytes 69287 | solution.py:40
  334.5 0.8 fusion.61
  336.0 0.8 fusion.61
  337.4 0.8 fusion.61
  338.9 0.8 fusion.61
  347.6 0.8 fusion.61
  349.0 0.8 fusion.61
  350.5 0.8 fusion.61
  351.9 0.8 fusion.61
  362.0 0.8 fusion.61
  363.5 0.8 fusion.61
  510.9 1.0 convolution_multiply_fusion.1
  511.9 126.9 %all-reduce.6.cloned.1.call-done = (f32[128,128]{1,0:T(8,128)}, f32[128,256]{1,0:T(8,128)}) async-done(((f32[128,128]{1,0:T(8,128)}, f32[128,256]{1,0:T(8,128)}), (f32[128,128]{1,0:T(8,128)}, f32[128,256]{1,0:T(8,128)})) %all-reduce.6.cloned.1.call-update) | async-done | bytes 196624 | tf_op jit(solution)/shard_map/psum | solution.py:54
  638.8 0.8 copy-done.2
  639.6 188.3 %while.90 = (s32[]{:T(128)}, f32[128,128]{1,0:T(8,128)S(1)}, f32[128,128]{1,0:T(8,128)S(1)}, s32[]{:T(128)}, s32[]{:T(128)}, /*index=5*/s32[]{:T(128)}) while((s32[]{:T(128)}, f32[128,128]{1,0:T(8,128)S(1)}, f32[128,128]{1,0:T(8,128)S(1)}, s32[]{:T(128)}, s32[]{:T(128)}, /*index=5*/s32[]{:T(128)}) %tuple.211), condition=%wide.region_7.8_spmd.clone, body=%wide.region_6.7_spmd.clone.sunk | while | flops 33667 | bytes 138357 | solution.py:24
  828.1 185.2 %while.88 = (s32[]{:T(128)}, f32[128,128]{1,0:T(8,128)S(1)}, f32[128,128]{1,0:T(8,128)S(1)}, f32[128,128]{1,0:T(8,128)S(1)}, s32[]{:T(128)}, /*index=5*/s32[]{:T(128)}, s32[]{:T(128)}, s32[]{:T(128)}) while((s32[]{:T(128)}, f32[128,128]{1,0:T(8,128)S(1)}, f32[128,128]{1,0:T(8,128)S(1)}, f32[128,128]{1,0:T(8,128)S(1)}, s32[]{:T(128)}, ...), condition=%wide.region_11.12_spmd, body=%wide.region_10.11_spmd.sunk | while | flops 196871 | bytes 69287 | solution.py:40
  1014.0 185.2 %while.87 = (s32[]{:T(128)}, f32[128,128]{1,0:T(8,128)S(1)}, f32[128,128]{1,0:T(8,128)S(1)}, f32[128,128]{1,0:T(8,128)S(1)}, s32[]{:T(128)}, /*index=5*/s32[]{:T(128)}, s32[]{:T(128)}, s32[]{:T(128)}) while((s32[]{:T(128)}, f32[128,128]{1,0:T(8,128)S(1)}, f32[128,128]{1,0:T(8,128)S(1)}, f32[128,128]{1,0:T(8,128)S(1)}, s32[]{:T(128)}, ...), condition=%wide.region_9.10_spmd, body=%wide.region_8.9_spmd.sunk | while | flops 196871 | bytes 69287 | solution.py:40
  1200.4 1.4 convolution_subtract_fusion
  (2705 shorter events, 725.2 us)
Async XLA Ops:
  7.2 1.0 copy-start
  7.2 2.2 copy-start.1
  7.2 128.9 %all-reduce.4.cloned.1.call-start = ((), (), s32[]{:S(2)}) async-start(), calls=%async_computation | async-start | bytes 131072 | tf_op jit(solution)/shard_map/psum | solution.py:51
  9.4 629.4 %all-reduce.6.cloned.1.call-start = ((), (), s32[]{:S(2)}) async-start(), calls=%async_computation.1 | async-start | bytes 393216 | tf_op jit(solution)/shard_map/psum | solution.py:54
  136.1 0.8 copy-start.3
  638.8 0.8 copy-start.2
  1013.3 0.6 copy-start.7
  1199.1 0.9 copy-start.6
  1199.7 2.0 copy-start.4
  1200.4 1.4 copy-start.5
Sparse Core Ops, SparseCore 0:
  14.2 121.9 all-reduce.3
  512.0 126.6 all-reduce.5
where the time goes:
time: 1220 us; the launch traced here: 1210 us
  local copies, waits for them, and re-layouts  401 us (33%)
  matrix products  313 us (26%)
  waiting for transfers between devices  252 us (21%)
  loops' own time  202 us (17%)
  other arithmetic  26.6 us (2%)
  between operations  14.2 us (1%)
    dot_general x384, matrix products, row_step(): partial_value = jnp.dot(upper_row, inverse, precision=lax.Precision.HIGHEST)  306 us
    dynamic_slice x384, local copies, waits for them, and re-layouts, row_step(): pivot = lax.dynamic_index_in_dim(upper_row, where, 0, keepdims=False)  226 us
    another operation x2, loops' own time, upper_factor(): return lax.fori_loop(0, order, column_step, start)[1]  190 us
    dynamic_slice x256, local copies, waits for them, and re-layouts, column_step(): pivot = lax.dynamic_index_in_dim(pivot_row, where, 0, keepdims=False)  151 us
    psum x1, waiting for transfers between devices, on_device(): lax.psum(product(basis_rows.T, basis_rows) / row_total, ('wide', 'narrow'))  127 us
    psum x1, waiting for transfers between devices, on_device(): lax.psum((gram_local, cross_local), ('wide', 'narrow'))  125 us
  transfers between devices with their start and end apart: 2, of which 2 were waited for; matrix products, arithmetic and copies ran while one was open for 0% of the time, Pallas kernels for 0%

commit v1 on v0

--- a/solution.py
+++ b/solution.py
@@ -51,7 +51,9 @@
     gram_first, cross_terms = lax.psum((gram_local, cross_local), ("wide", "narrow"))
     first_factor = upper_factor(gram_first)
     basis_rows = product(panel, inverse_upper(first_factor))
-    gram_second = lax.psum(product(basis_rows.T, basis_rows) / row_total, ("wide", "narrow"))
+    gram_second = jnp.sum(
+        lax.all_gather(product(basis_rows.T, basis_rows) / row_total, ("wide", "narrow")), axis=0
+    )
     second_factor = upper_factor(gram_second)
     q_factor = product(basis_rows, inverse_upper(second_factor))
     r_factor = product(second_factor, first_factor)

time: 1220 us -> 1520 us (1.25)
  other arithmetic: 26.6 us -> 302 us
  local copies, waits for them, and re-layouts: 401 us -> 484 us
  waiting for transfers between devices: 252 us -> 185 us
    sub x256, other arithmetic: 21 us -> 208 us  [column_step(): work = work - new_row[:, None] * new_row[None, :]]
    psum x1 -> x0, waiting for transfers between devices: 127 us -> none  [on_device(): lax.psum(product(basis_rows.T, basis_rows) / row_total, ('wide', 'narrow'))]
    select_n x512, other arithmetic: 4.58 us -> 91.5 us  [column_step(): jnp.where(columns >= where, pivot_row / jnp.sqrt(pivot), jnp.zeros_like(p...]
    dynamic_slice x256, local copies, waits for them, and re-layouts: 151 us -> 237 us  [column_step(): pivot = lax.dynamic_index_in_dim(pivot_row, where, 0, keepdims=False)]
    all_gather x0 -> x1, waiting for transfers between devices: none -> 54.5 us  [on_device(): lax.all_gather(product(basis_rows.T, basis_rows) / row_total, ('wide', 'n...]
where the time goes in v1:
time: 1520 us; the launch traced here: 1500 us
  local copies, waits for them, and re-layouts  484 us (32%)
  matrix products  314 us (21%)
  other arithmetic  302 us (20%)
  loops' own time  197 us (13%)
  waiting for transfers between devices  185 us (12%)
    dot_general x384, matrix products, row_step(): partial_value = jnp.dot(upper_row, inverse, precision=lax.Precision.HIGHEST)  306 us
    dynamic_slice x256, local copies, waits for them, and re-layouts, column_step(): pivot = lax.dynamic_index_in_dim(pivot_row, where, 0, keepdims=False)  237 us
    dynamic_slice x384, local copies, waits for them, and re-layouts, row_step(): pivot = lax.dynamic_index_in_dim(upper_row, where, 0, keepdims=False)  226 us
    sub x256, other arithmetic, column_step(): work = work - new_row[:, None] * new_row[None, :]  208 us
    another operation x2, loops' own time, upper_factor(): return lax.fori_loop(0, order, column_step, start)[1]  185 us
    psum x1, waiting for transfers between devices, on_device(): lax.psum((gram_local, cross_local), ('wide', 'narrow'))  130 us
    select_n x512, other arithmetic, column_step(): jnp.where(columns >= where, pivot_row / jnp.sqrt(pivot), jnp.zeros_like(p...  91.5 us
    all_gather x1, waiting for transfers between devices, on_device(): lax.all_gather(product(basis_rows.T, basis_rows) / row_total, ('wide', 'n...  54.5 us
  transfers between devices with their start and end apart: 2, of which 2 were waited for; matrix products, arithmetic and copies ran while one was open for 0% of the time, Pallas kernels for 0%

profile of v1, /device:TPU:8, one launch (start us, length us, event | category | flops | bytes accessed | tf_op | source)
XLA Modules:
  0.0 1495.1 jit_solution(8024177847361000524)
XLA Ops:
  9.3 2.3 convolution_multiply_fusion
  11.7 130.5 %all-reduce.3.cloned.1.call-done = (f32[128,128]{1,0:T(8,128)}, f32[128,256]{1,0:T(8,128)}) async-done(((f32[128,128]{1,0:T(8,128)}, f32[128,256]{1,0:T(8,128)}), (f32[128,128]{1,0:T(8,128)}, f32[128,256]{1,0:T(8,128)})) %all-reduce.3.cloned.1.call-update) | async-done | bytes 196624 | tf_op jit(solution)/shard_map/psum | solution.py:51
  142.2 542.0 %while.89 = (s32[]{:T(128)}, f32[128,128]{1,0:T(8,128)}, f32[128,128]{1,0:T(8,128)S(1)}, s32[]{:T(128)}, s32[]{:T(128)}, /*index=5*/s32[]{:T(128)}) while((s32[]{:T(128)}, f32[128,128]{1,0:T(8,128)}, f32[128,128]{1,0:T(8,128)S(1)}, s32[]{:T(128)}, s32[]{:T(128)}, /*index=5*/s32[]{:T(128)}) %tuple.191), condition=%wide.region_2.3_spmd.clone, body=%wide.region_1.0_spmd.clone.sunk | while | flops 33667 | bytes 138357 | solution.py:24
  149.1 1.5 multiply_subtract_fusion.4
  157.6 1.5 multiply_subtract_fusion.4
  178.7 1.5 multiply_subtract_fusion.4
  212.5 1.5 multiply_subtract_fusion.4
  229.5 1.5 multiply_subtract_fusion.4
  242.2 1.5 multiply_subtract_fusion.4
  263.4 1.5 multiply_subtract_fusion.4
  276.1 1.5 multiply_subtract_fusion.4
  293.1 1.5 multiply_subtract_fusion.4
  297.4 1.5 multiply_subtract_fusion.4
  314.3 1.5 multiply_subtract_fusion.4
  331.3 1.5 multiply_subtract_fusion.4
  386.2 1.5 multiply_subtract_fusion.4
  407.4 1.5 multiply_subtract_fusion.4
  428.6 1.5 multiply_subtract_fusion.4
  684.2 185.2 %while.86 = (s32[]{:T(128)}, f32[128,128]{1,0:T(8,128)S(1)}, f32[128,128]{1,0:T(8,128)S(1)}, f32[128,128]{1,0:T(8,128)S(1)}, s32[]{:T(128)}, /*index=5*/s32[]{:T(128)}, s32[]{:T(128)}, s32[]{:T(128)}) while((s32[]{:T(128)}, f32[128,128]{1,0:T(8,128)S(1)}, f32[128,128]{1,0:T(8,128)S(1)}, f32[128,128]{1,0:T(8,128)S(1)}, s32[]{:T(128)}, ...), condition=%wide.region_4.5_spmd, body=%wide.region_3.4_spmd.sunk | while | flops 196871 | bytes 69287 | solution.py:40
  870.8 54.5 %all-gather.3.cloned.1.call-done = f32[4096,128]{1,0:T(8,128)} async-done(((f32[128,128]{1,0:T(8,128)}), f32[4096,128]{1,0:T(8,128)}) %all-gather.3.cloned.1.call-update) | async-done | bytes 2097168 | tf_op jit(solution)/shard_map/all_gather | solution.py:55
  925.3 1.7 reduce_sum.9
  927.1 188.3 %while.90 = (s32[]{:T(128)}, f32[128,128]{1,0:T(8,128)S(1)}, f32[128,128]{1,0:T(8,128)S(1)}, s32[]{:T(128)}, s32[]{:T(128)}, /*index=5*/s32[]{:T(128)}) while((s32[]{:T(128)}, f32[128,128]{1,0:T(8,128)S(1)}, f32[128,128]{1,0:T(8,128)S(1)}, s32[]{:T(128)}, s32[]{:T(128)}, /*index=5*/s32[]{:T(128)}) %tuple.197), condition=%wide.region_7.8_spmd.clone, body=%wide.region_6.7_spmd.clone.sunk | while | flops 33667 | bytes 138357 | solution.py:24
  1115.6 185.2 %while.87 = (s32[]{:T(128)}, f32[128,128]{1,0:T(8,128)S(1)}, f32[128,128]{1,0:T(8,128)S(1)}, f32[128,128]{1,0:T(8,128)S(1)}, s32[]{:T(128)}, /*index=5*/s32[]{:T(128)}, s32[]{:T(128)}, s32[]{:T(128)}) while((s32[]{:T(128)}, f32[128,128]{1,0:T(8,128)S(1)}, f32[128,128]{1,0:T(8,128)S(1)}, f32[128,128]{1,0:T(8,128)S(1)}, s32[]{:T(128)}, ...), condition=%wide.region_9.10_spmd, body=%wide.region_8.9_spmd.sunk | while | flops 196871 | bytes 69287 | solution.py:40
  1301.4 185.1 %while.88 = (s32[]{:T(128)}, f32[128,128]{1,0:T(8,128)S(1)}, f32[128,128]{1,0:T(8,128)S(1)}, f32[128,128]{1,0:T(8,128)S(1)}, s32[]{:T(128)}, /*index=5*/s32[]{:T(128)}, s32[]{:T(128)}, s32[]{:T(128)}) while((s32[]{:T(128)}, f32[128,128]{1,0:T(8,128)S(1)}, f32[128,128]{1,0:T(8,128)S(1)}, f32[128,128]{1,0:T(8,128)S(1)}, s32[]{:T(128)}, ...), condition=%wide.region_11.12_spmd, body=%wide.region_10.11_spmd.sunk | while | flops 196871 | bytes 69287 | solution.py:40
  (2702 shorter events, 1072.3 us)
Async XLA Ops:
  7.2 1.0 copy-start
  7.2 135.0 %all-reduce.3.cloned.1.call-start = ((), (), s32[]{:S(2)}) async-start(), calls=%async_computation.1 | async-start | bytes 393216 | tf_op jit(solution)/shard_map/psum | solution.py:51
  11.7 913.6 %all-gather.3.cloned.1.call-start = ((), (), s32[]{:S(2)}) async-start(), calls=%async_computation | async-start | bytes 2162688 | tf_op jit(solution)/shard_map/all_gather | solution.py:55
  925.3 561.3 %copy-start.4 = (f32[128,256]{1,0:T(8,128)S(1)}, f32[128,256]{1,0:T(8,128)}, u32[]{:S(2)}) copy-start(f32[128,256]{1,0:T(8,128)} %get-tuple-element.691) | copy-start | bytes 393220
  927.0 559.8 %copy-start.1 = (f32[512,256]{1,0:T(8,128)S(1)}, f32[512,256]{1,0:T(8,128)}, u32[]{:S(2)}) copy-start(f32[512,256]{1,0:T(8,128)} %param.13) | copy-start | bytes 1572868
  1301.4 186.9 %copy-start.2 = (f32[512,128]{1,0:T(8,128)}, f32[512,128]{1,0:T(8,128)S(1)}, u32[]{:S(2)}) copy-start(f32[512,128]{1,0:T(8,128)S(1)} %fusion.24) | copy-start | bytes 786436
  1486.6 1.7 copy-start.5
  1486.9 1.4 copy-start.3
Sparse Core Ops, SparseCore 0:
  14.2 127.9 all-reduce.2
  871.0 54.2 all-gather.2
